TPU v7x, 512 devices: a whole 4x8x8 slice. The times are simulated.
512 devices in a mesh: grp: 32 (over z, x), vox: 16 (over y, core).
Axes of the slice: x: 4, y: 8, z: 8, core: 2. Of those that a mesh axis runs over, the one named last changes fastest.
Arguments:
- group_basis: bfloat16 [32, 16384, 256], P('grp', 'vox'), may hold values from -6 to 6
- timeseries: bfloat16 [32, 16384, 512], P('grp', 'vox'), may hold values from -6 to 6
Outputs:
- loadings: float32 [32, 256, 512], P('grp', 'vox')
All inputs are finite; a program needn't handle non-finite values.
Results may differ from a plain program's by a relative error of at most 0.015.
Values may be sent and summed in bfloat16 or wider, within the bound.
No kernel may reach another device: no remote copies, remote signals or barrier semaphores. Data moves between devices by JAX's collectives and lax.ppermute only.
A program may use at most 64 MiB of HBM per device.

v0:
```python
import functools

import jax
import jax.numpy as jnp
from jax import lax
from jax.experimental import pallas as pl
from jax.experimental.pallas import tpu as pltpu
from jax.sharding import PartitionSpec as P


N = 256
H = 128
VOX = 16
GRP = 32
ROWS = N // VOX
F32 = jnp.float32
BF16 = jnp.bfloat16

NN = (((1,), (0,)), ((), ()))
NT = (((1,), (1,)), ((), ()))
VMEM = pl.BlockSpec(memory_space=pltpu.VMEM)
SMEM = pl.BlockSpec(memory_space=pltpu.SMEM)
HBM = pl.BlockSpec(memory_space=pltpu.MemorySpace.HBM)


def params(mib):
    return pltpu.CompilerParams(vmem_limit_bytes=mib << 20)


def dot1(a, b, dims):
    return lax.dot_general(a.astype(BF16), b.astype(BF16), dims, preferred_element_type=F32)


def split(x):
    hi = x.astype(BF16)
    return hi, (x - hi.astype(F32)).astype(BF16)


def dot3(a, b, dims):
    dot = functools.partial(lax.dot_general, dimension_numbers=dims, preferred_element_type=F32)
    return dot(a[0], b[0]) + (dot(a[0], b[1]) + dot(a[1], b[0]))


def dot_full(a, b, dims):
    return lax.dot_general(a, b, dims, preferred_element_type=F32, precision=lax.Precision.HIGHEST)


def iotas():
    shape = (N, N)
    return lax.broadcasted_iota(jnp.int32, shape, 0), lax.broadcasted_iota(jnp.int32, shape, 1)


def inv_sqrt_diag(m, eye):
    picked = jnp.where(eye, m, 0.0)
    col = lax.rsqrt(jnp.sum(picked, axis=1, keepdims=True))
    row = lax.rsqrt(jnp.sum(picked, axis=0, keepdims=True))
    return col, row


def inverse_factor(m, steps):
    r, c = iotas()
    eye = r == c
    below = r > c
    one = jnp.where(eye, 1.0, 0.0)
    col, start = inv_sqrt_diag(m, eye)
    m = col * m * start
    s = jnp.where(below, m, 0.0)
    s2 = dot1(s, s, NN)
    t = one - s
    x = t + dot1(t, s2, NN)
    for _ in range(steps):
        mk = dot1(dot1(x, m, NN), x, NT)
        col, row = inv_sqrt_diag(mk, eye)
        s = jnp.where(below, col * mk * row, 0.0)
        s2 = dot1(s, s, NN)
        t = one - s
        x = col * x
        x = x - dot1(s, x, NN) + dot1(dot1(t, s2, NN), x, NN)
    x = jnp.where(r >= c, x, 0.0)
    xs = split(x)
    mk = dot3(split(dot3(xs, split(m), NN)), xs, NT)
    col, row = inv_sqrt_diag(mk, eye)
    off = jnp.where(eye, 0.0, col * mk * row)
    size = jnp.sum(off * off)
    s = jnp.where(below, off, 0.0)
    x = col * x
    step = s - dot1(s, s, NN)
    x = x - dot3(split(step), split(x), NN)
    return x * start, size


def factor_columns(m_ref, l_ref):
    r, c = iotas()

    def body(j, _):
        m = m_ref[...]
        row = jnp.sum(jnp.where(r == j, m, 0.0), axis=0, keepdims=True)
        col = jnp.sum(jnp.where(c == j, m, 0.0), axis=1, keepdims=True)
        pivot = jnp.sum(jnp.where((r == j) & (c == j), m, 0.0))
        pivot = jnp.full((1, N), pivot, F32)
        row = jnp.where(c[:1] >= j, row, 0.0)
        col = jnp.where(r[:, :1] >= j, col, 0.0)
        m_ref[...] = m - col * (row / pivot)
        l_ref[...] = jnp.where(c == j, col / jnp.sqrt(pivot), l_ref[...])
        return 0

    lax.fori_loop(0, N, body, 0)


def invert_lower(l_ref, x_ref):
    r, c = iotas()
    eye = r == c
    diag = jnp.sum(jnp.where(eye, l_ref[...], 0.0), axis=1, keepdims=True)
    x_ref[...] = jnp.where(eye, 1.0 / diag, 0.0)

    def body(k, _):
        rk, ck = r >> k, c >> k
        off = jnp.where(((rk >> 1) == (ck >> 1)) & (rk > ck), l_ref[...], 0.0)
        x = x_ref[...]
        x_ref[...] = x - dot_full(dot_full(x, off, NN), x, NN)
        return 0

    lax.fori_loop(0, 8, body, 0)


def weights_body(a, b, cross, out_ref, y_ref, z_ref, m_ref, l_ref):
    plain = a is None
    r, c = iotas()
    if plain:
        one = jnp.where(r == c, 1.0, 0.0)
        t0, t1 = one + cross.T, one + cross
        unscale = 1.0
    else:
        top = jnp.max(jnp.where(r == c, jnp.maximum(a, b), 0.0))
        top = jnp.full((1, N), top, F32)
        inv = 1.0 / top
        unscale = lax.rsqrt(top)
        a, b, cross = a * inv, b * inv, cross * inv
        sa, sb, sc = split(a), split(b), split(cross)
        t0, t1 = a + cross.T, b + cross

    def times(t0, t1):
        s0, s1 = split(t0), split(t1)
        if plain:
            left = dot1(s1[0], cross, NT) + dot1(s1[1], cross, NT)
            right = dot1(s0[0], cross, NN) + dot1(s0[1], cross, NN)
            return t0 + left, t1 + right
        left, right = dot3(s1, sc, NT), dot3(s0, sc, NN)
        return dot3(s0, sa, NN) + left, dot3(s1, sb, NN) + right

    u0, u1 = times(t0, t1)
    v0, v1 = times(u0, u1)
    us0, us1 = split(u0), split(u1)
    m = dot3(split(v0), us0, NT) + dot3(split(v1), us1, NT)
    x, size = inverse_factor(m, 1 if plain else 2)
    xs = split(x)
    out_ref[0] = (dot3(xs, us0, NN) * unscale).astype(BF16)
    out_ref[1] = (dot3(xs, us1, NN) * unscale).astype(BF16)
    good = jnp.where(size < 0.06, 1, 0)

    @pl.when(good == 0)
    def _():
        y_ref[0] = t0
        y_ref[1] = t1

        def step(it, _):
            y0, y1 = y_ref[0], y_ref[1]
            left, right = dot_full(y1, cross, NT), dot_full(y0, cross, NN)
            if plain:
                z0, z1 = y0 + left, y1 + right
            else:
                z0, z1 = dot_full(y0, a, NN) + left, dot_full(y1, b, NN) + right
            m_ref[...] = dot_full(z0, y0, NT) + dot_full(z1, y1, NT)
            z_ref[0] = jnp.where(it == 0, z0, y0)
            z_ref[1] = jnp.where(it == 0, z1, y1)
            l_ref[...] = jnp.zeros((N, N), F32)
            factor_columns(m_ref, l_ref)
            invert_lower(l_ref, m_ref)
            xi = m_ref[...]
            y_ref[0] = dot_full(xi, z_ref[0], NN)
            y_ref[1] = dot_full(xi, z_ref[1], NN)
            return 0

        lax.fori_loop(0, 2, step, 0)
        out_ref[0] = (y_ref[0] * unscale).astype(BF16)
        out_ref[1] = (y_ref[1] * unscale).astype(BF16)


def mixed(p_ref, q_ref, w_ref):
    out = dot1(p_ref[...], w_ref[0], NT) + dot1(q_ref[...], w_ref[1], NT)
    return out.astype(BF16)


def mixed_turned(p_ref, q_ref, w_ref):
    out = dot1(w_ref[0], p_ref[...], NT) + dot1(w_ref[1], q_ref[...], NT)
    return out.astype(BF16)


def send_products(turned, sides, proj_hbm, proj_ref, sems):
    copies = []
    for k, side in enumerate(sides):
        got = dot1(turned, side[...], NN).astype(BF16)
        at = pl.ds(N * k, N)
        proj_ref[:, :, N * k : N * (k + 1)] = got.reshape(VOX, ROWS, N)
        copies.append(pltpu.make_async_copy(proj_ref.at[:, :, at], proj_hbm.at[:, :, at], sems.at[k]))
        copies[-1].start()
    for copy in copies:
        copy.wait()


PARTS = jax.ShapeDtypeStruct((VOX, ROWS, 2 * N), BF16)
SENDING = [pltpu.VMEM(PARTS.shape, BF16), pltpu.SemaphoreType.DMA((2,))]
SCRATCH = [pltpu.VMEM((2, N, N), F32)] * 2 + [pltpu.VMEM((N, N), F32)] * 2
WEIGHTS = jax.ShapeDtypeStruct((2, N, N), BF16)


def full_kernel(core_ref, mine_ref, theirs_ref, p_ref, q_ref, r_ref, s_ref, *refs):
    out_ref, node_hbm, proj_hbm, a_ref, c_ref = refs[:5]
    core = core_ref[0]
    for half, ref in ((core, mine_ref), (1 - core, theirs_ref)):
        for y in range(8):
            block = 2 * y + half
            lo = pl.ds(pl.multiple_of(8 * block, 8), 8)
            hi = pl.ds(pl.multiple_of(H + 8 * block, 8), 8)
            for k in range(2):
                a_ref[k, lo, :H] = ref[y, 24 * k : 24 * k + 8, :]
                a_ref[k, hi, H:] = ref[y, 24 * k + 8 : 24 * k + 16, :]
                a_ref[k, hi, :H] = ref[y, 24 * k + 16 : 24 * k + 24, :]
            at = pl.ds(pl.multiple_of(ROWS * block, ROWS), ROWS)
            c_ref[at, :H] = ref[y, 48:64, :]
            c_ref[at, H:] = ref[y, 64:80, :]
    for k in range(2):
        a_ref[k, :H, H:] = a_ref[k, H:, :H].T
    node_ref, sem = refs[5:7]
    weights_body(a_ref[0], a_ref[1], c_ref[...], out_ref, *refs[9:])
    node_ref[...] = mixed(p_ref, q_ref, out_ref)
    copy = pltpu.make_async_copy(node_ref, node_hbm, sem)
    copy.start()
    turned = mixed_turned(p_ref, q_ref, out_ref)
    send_products(turned, (r_ref, s_ref), proj_hbm, *refs[7:9])
    copy.wait()


def full_merge(core, mine, theirs, p, q, r, s):
    return pl.pallas_call(
        full_kernel,
        out_shape=(WEIGHTS, jax.ShapeDtypeStruct(p.shape, BF16), PARTS),
        in_specs=[SMEM] + [VMEM] * 6,
        out_specs=(VMEM, HBM, HBM),
        scratch_shapes=[pltpu.VMEM((2, N, N), F32), pltpu.VMEM((N, N), F32)]
        + [pltpu.VMEM(p.shape, BF16), pltpu.SemaphoreType.DMA]
        + SENDING
        + SCRATCH,
        compiler_params=params(16),
        name="full_merge",
    )(core, mine, theirs, p, q, r, s)


def plain_kernel(cross_ref, p_hbm, q_ref, out_ref, turned_ref, p_ref, sem, *scratch):
    copy = pltpu.make_async_copy(p_hbm, p_ref, sem)
    copy.start()
    weights_body(None, None, cross_ref[...].astype(F32), out_ref, *scratch)
    copy.wait()
    turned_ref[...] = mixed_turned(p_ref, q_ref, out_ref)


def plain_merge(cross, p, q):
    return pl.pallas_call(
        plain_kernel,
        out_shape=(WEIGHTS, jax.ShapeDtypeStruct(p.shape[::-1], BF16)),
        in_specs=[VMEM, HBM, VMEM],
        out_specs=(VMEM, VMEM),
        scratch_shapes=[pltpu.VMEM(p.shape, BF16), pltpu.SemaphoreType.DMA] + SCRATCH,
        compiler_params=params(14),
        name="plain_merge",
    )(cross, p, q)


def mix_kernel(p_ref, q_ref, w_ref, out_ref):
    out_ref[...] = mixed(p_ref, q_ref, w_ref)


def mix(p, q, w):
    return pl.pallas_call(
        mix_kernel,
        out_shape=jax.ShapeDtypeStruct(p.shape, BF16),
        in_specs=[VMEM] * 3,
        out_specs=VMEM,
        compiler_params=params(6),
        name="mix",
    )(p, q, w)


def project_kernel(turned_ref, r_ref, s_ref, proj_hbm, *refs):
    send_products(turned_ref[...], (r_ref, s_ref), proj_hbm, *refs)


def project(turned, r, s):
    return pl.pallas_call(
        project_kernel,
        out_shape=PARTS,
        in_specs=[VMEM] * 3,
        out_specs=HBM,
        scratch_shapes=SENDING,
        compiler_params=params(8),
        name="project",
    )(turned, r, s)


def last_kernel(cross_ref, turned_hbm, q_ref, series_hbm, out_ref, *refs):
    turned_ref, series_ref, first_sem, second_sem, w_ref = refs[:5]
    first = pltpu.make_async_copy(turned_hbm, turned_ref, first_sem)
    first.start()
    second = pltpu.make_async_copy(series_hbm, series_ref, second_sem)
    second.start()
    weights_body(None, None, cross_ref[...].astype(F32), w_ref, *refs[5:])
    first.wait()
    second.wait()
    root = dot1(w_ref[0], turned_ref[...], NN) + dot1(w_ref[1], q_ref[...], NT)
    out_ref[...] = dot1(root, series_ref[...], NN).astype(BF16).reshape(out_ref.shape)


def last_merge(cross, turned, q, series):
    return pl.pallas_call(
        last_kernel,
        out_shape=jax.ShapeDtypeStruct((VOX, ROWS, series.shape[1]), BF16),
        in_specs=[VMEM, HBM, VMEM, HBM],
        out_specs=VMEM,
        scratch_shapes=[pltpu.VMEM(turned.shape, BF16), pltpu.VMEM(series.shape, BF16)]
        + [pltpu.SemaphoreType.DMA] * 2
        + [pltpu.VMEM((2, N, N), BF16)]
        + SCRATCH,
        compiler_params=params(16),
        name="last_merge",
    )(cross, turned, q, pltpu.with_memory_space_constraint(series, pltpu.MemorySpace.HBM))


def lower_blocks(p, q):
    pairs = ((0, 0), (1, 1), (1, 0))
    half = lambda k: slice(H * k, H * (k + 1))
    return [dot1(p[half(i), :], q[:, half(j)], NN) for i, j in pairs]


def self_gram_kernel(p_hbm, turned_ref, out_ref, p_ref, sem):
    copy = pltpu.make_async_copy(p_hbm, p_ref, sem)
    copy.start()
    copy.wait()
    p = p_ref[...]
    turned = p.T
    turned_ref[...] = turned
    for k, block in enumerate(lower_blocks(turned, p)):
        out_ref[:, 8 * k : 8 * k + 8, :] = block.astype(BF16).reshape(VOX, 8, H)


def self_gram(p):
    return pl.pallas_call(
        self_gram_kernel,
        out_shape=(
            jax.ShapeDtypeStruct(p.shape[::-1], BF16),
            jax.ShapeDtypeStruct((VOX, 24, H), BF16),
        ),
        in_specs=[HBM],
        out_specs=(VMEM, VMEM),
        scratch_shapes=[pltpu.VMEM(p.shape, BF16), pltpu.SemaphoreType.DMA],
        compiler_params=params(6),
        name="self_gram",
    )(pltpu.with_memory_space_constraint(p, pltpu.MemorySpace.HBM))


def pair_gram_kernel(turned_ref, q_ref, own_ref, out_ref):
    q = q_ref[...]
    out_ref[:, :24, :] = own_ref[...]
    for k, block in enumerate(lower_blocks(q.T, q)):
        out_ref[:, 24 + 8 * k : 32 + 8 * k, :] = block.astype(BF16).reshape(VOX, 8, H)
    for k in range(2):
        got = dot1(turned_ref[...], q[:, H * k : H * (k + 1)], NN).astype(BF16)
        out_ref[:, 48 + ROWS * k : 64 + ROWS * k, :] = got.reshape(VOX, ROWS, H)


def pair_gram(turned, q, own):
    return pl.pallas_call(
        pair_gram_kernel,
        out_shape=jax.ShapeDtypeStruct((VOX, 80, H), BF16),
        in_specs=[VMEM] * 3,
        out_specs=VMEM,
        compiler_params=params(8),
        name="pair_gram",
    )(turned, q, own)


def rows_kernel(parts_ref, w_ref, out_ref):
    total = jnp.sum(parts_ref[...].astype(F32), axis=0)
    hi, lo = split(total)
    got = jnp.zeros((ROWS, N), F32)
    for k in range(2):
        at = slice(N * k, N * (k + 1))
        got = got + (dot1(hi[:, at], w_ref[k], NT) + dot1(lo[:, at], w_ref[k], NT))
    out_ref[...] = jnp.broadcast_to(got.astype(BF16)[None], out_ref.shape)


def cross_rows_of(parts, w):
    return pl.pallas_call(
        rows_kernel,
        out_shape=jax.ShapeDtypeStruct((VOX, ROWS, N), BF16),
        in_specs=[VMEM, VMEM],
        out_specs=VMEM,
        compiler_params=params(4),
        name="cross_rows",
    )(parts, w)


def partner(value, mask):
    return lax.ppermute(value, "grp", [(g, g ^ mask) for g in range(GRP)])


def exchange(parts):
    return lax.all_to_all(parts, "vox", 0, 0)


def same_core(rows):
    groups = [[2 * y + c for y in range(8)] for c in range(2)]
    sent = jnp.broadcast_to(rows[None], (8,) + rows.shape)
    return lax.all_to_all(sent, "vox", 0, 0, axis_index_groups=groups)


def swap_cores(value):
    return lax.ppermute(value, "vox", [(v, v ^ 1) for v in range(VOX)])


def add_up(parts):
    return jnp.sum(parts.astype(F32), axis=0)


def tree(own, series):
    core = (lax.axis_index("vox") & 1).astype(jnp.int32).reshape(1)
    other = partner(own, 1)
    turned, own_parts = self_gram(own)
    far_own = partner(own, 3)
    far_other = partner(other, 3)
    parts = pair_gram(turned, other, own_parts)
    rows = add_up(exchange(parts))
    mine = same_core(rows)
    theirs = swap_cores(mine)
    w, left, parts = full_merge(core, mine, theirs, own, other, far_own, far_other)
    parts = exchange(parts)
    far_w = partner(w, 3)
    deep_left = partner(left, 4)
    deep_right = partner(left, 7)
    cross = exchange(cross_rows_of(parts, far_w))
    right = mix(far_own, far_other, far_w)
    w, turned = plain_merge(cross.reshape(N, N), left, right)

    parts = project(turned, deep_left, deep_right)
    parts = exchange(parts)
    deep_w = partner(w, 4)
    cross = exchange(cross_rows_of(parts, deep_w))
    right = mix(deep_left, deep_right, deep_w)
    parts = last_merge(cross.reshape(N, N), turned, right, series)
    return add_up(exchange(parts))


def local(group_basis, timeseries):
    return tree(group_basis[0], timeseries[0])[None]


def solution(mesh):
    return jax.shard_map(
        local,
        mesh=mesh,
        in_specs=(P("grp", "vox", None), P("grp", "vox", None)),
        out_specs=P("grp", "vox", None),
        check_vma=False,
    )
```

profile of v0, /device:TPU:1, one launch (start us, length us, event | category | flops | bytes accessed | tf_op | source)
XLA Modules:
  0.0 338.6 jit_solution(17141242148177861665)
XLA Ops:
  0.0 3.9 %collective-permute-start = (bf16[1024,256]{1,0:T(8,128)(2,1)}, bf16[1024,256]{1,0:T(8,128)(2,1)S(1)}, u32[]{:S(2)}, u32[]{:S(2)}) collective-permute-start(bf16[1024,256]{1,0:T(8,128)(2,1)} %bitcast.6), channel_id=1, source_target_pairs={{0,16},{16,0},{32,48},{48,32},{64,80},{80,64},{96,112},{112,96},{1... | collective-permute-start | bytes 1572872 | tf_op jit(solution)/shard_map/ppermute | solution.py:413
  3.9 1.5 self_gram.1
  5.4 5.6 %collective-permute-done.q_ref = bf16[1024,256]{1,0:T(8,128)(2,1)S(1)} collective-permute-done((bf16[1024,256]{1,0:T(8,128)(2,1)}, bf16[1024,256]{1,0:T(8,128)(2,1)S(1)}, u32[]{:S(2)}, u32[]{:S(2)}) %collective-permute-start) | collective-permute-done | bytes 524320 | tf_op jit(solution)/shard_map/ppermute | solution.py:413
  11.0 0.7 pair_gram.1
  11.7 26.2 %all_to_all.35 = bf16[16,80,128]{2,1,0:T(8,128)(2,1)S(1)} all-to-all(bf16[16,80,128]{2,1,0:T(8,128)(2,1)S(1)} %pair_gram.1), channel_id=1, replica_groups=mesh['grp'=32,'vox'=16] {'vox'}, dimensions={0} | all-to-all | bytes 655360 | tf_op jit(solution)/shard_map/all_to_all | solution.py:417
  37.8 0.1 convert_reduce_fusion
  37.9 0.0 copy-start
  37.9 0.7 broadcast_in_dim.4
  38.6 3.4 %all-to-all-start.1 = ((f32[8,80,128]{2,1,0:T(8,128)}), f32[8,80,128]{2,1,0:T(8,128)S(1)}, u32[]{:S(2)}, u32[]{:S(2)}) async-start(f32[8,80,128]{2,1,0:T(8,128)} %broadcast_in_dim.4), calls=%async_computation.1 | async-start | bytes 655360 | tf_op jit(solution)/shard_map/all_to_all | solution.py:423
  42.1 0.0 copy-done
  42.1 4.4 %collective-permute-start.2 = (bf16[1024,256]{1,0:T(8,128)(2,1)S(1)}, bf16[1024,256]{1,0:T(8,128)(2,1)S(1)}, u32[]{:S(2)}, u32[]{:S(2)}) collective-permute-start(bf16[1024,256]{1,0:T(8,128)(2,1)S(1)} %bitcast.8), channel_id=1, source_target_pairs={{0,48},{16,32},{32,16},{48,0},{64,112},{80,96},{96,80},{112,64},{1... | collective-permute-start | bytes 1572872 | tf_op jit(solution)/shard_map/ppermute | solution.py:413
  46.5 2.1 collective-permute-start.3
  48.6 7.2 %all-to-all-done.1.mine_ref = f32[8,80,128]{2,1,0:T(8,128)S(1)} async-done(((f32[8,80,128]{2,1,0:T(8,128)}), f32[8,80,128]{2,1,0:T(8,128)S(1)}, u32[]{:S(2)}, u32[]{:S(2)}) %all-to-all-start.1) | async-done | bytes 327712 | tf_op jit(solution)/shard_map/all_to_all | solution.py:423
  55.8 2.3 collective-permute-start.1
  58.1 1.0 collective-permute-done.2.r_ref.p_ref
  59.1 11.2 %collective-permute-done.3.s_ref.q_ref = bf16[1024,256]{1,0:T(8,128)(2,1)S(1)} collective-permute-done((bf16[1024,256]{1,0:T(8,128)(2,1)S(1)}, bf16[1024,256]{1,0:T(8,128)(2,1)S(1)}, u32[]{:S(2)}, u32[]{:S(2)}) %collective-permute-start.3) | collective-permute-done | bytes 524320 | tf_op jit(solution)/shard_map/ppermute | solution.py:413
  70.3 0.0 collective-permute-done.1.theirs_ref
  70.3 162.6 %full_merge.1 = (bf16[2,256,256]{2,1,0:T(8,128)(2,1)S(1)}, bf16[1024,256]{1,0:T(8,128)(2,1)S(1)}, bf16[16,16,512]{2,1,0:T(8,128)(2,1)S(1)}) custom-call(s32[1]{0:T(128)} %bitcast.core_ref, f32[8,80,128]{2,1,0:T(8,128)S(1)} %all-to-all-done.1.mine_ref, f32[8,80,128]{2,1,0:T(8,128)S(1)} %collective-permute-done.1.theirs_ref, bf16[1024,256]{1,0:T(8,128)(2,1)S(1)} %bitcast.9, ...), custom_call_target="tpu_custom_call" | custom-call | tf_op jit(solution)/shard_map/full_merge/pallas_call | solution.py:245
  233.0 0.0 copy-start.1
  233.0 0.7 copy-done.1
  233.7 0.0 copy-start.2
  233.7 0.7 copy-done.2
  234.4 7.4 %all-to-all-start.2 = ((bf16[16,16,512]{2,1,0:T(8,128)(2,1)}), bf16[16,16,512]{2,1,0:T(8,128)(2,1)S(1)}, u32[]{:S(2)}, u32[]{:S(2)}) async-start(bf16[16,16,512]{2,1,0:T(8,128)(2,1)} %copy-done.1), calls=%async_computation.2 | async-start | bytes 524288 | tf_op jit(solution)/shard_map/all_to_all | solution.py:417
  241.8 6.2 %collective-permute-start.6 = (bf16[1024,256]{1,0:T(8,128)(2,1)S(1)}, bf16[1024,256]{1,0:T(8,128)(2,1)S(1)}, u32[]{:S(2)}, u32[]{:S(2)}) collective-permute-start(bf16[1024,256]{1,0:T(8,128)(2,1)S(1)} %get-tuple-element.16.p_hbm), channel_id=1, source_target_pairs={{0,112},{16,96},{32,80},{48,64},{64,48},{80,32},{96,16},{112,0},{1... | collective-permute-start | bytes 1572872 | tf_op jit(solution)/shard_map/ppermute | solution.py:413
  248.0 1.9 collective-permute-start.5
  249.9 0.0 copy-done.3
  249.9 2.2 collective-permute-start.4
  252.1 13.9 %collective-permute-done.4.w_ref = bf16[2,256,256]{2,1,0:T(8,128)(2,1)S(1)} collective-permute-done((bf16[2,256,256]{2,1,0:T(8,128)(2,1)S(1)}, bf16[2,256,256]{2,1,0:T(8,128)(2,1)S(1)}, u32[]{:S(2)}, u32[]{:S(2)}) %collective-permute-start.4) | collective-permute-done | bytes 262176 | tf_op jit(solution)/shard_map/ppermute | solution.py:413
  266.0 0.0 all-to-all-done.2.parts_ref
  266.0 0.9 cross_rows.2
  266.9 7.3 %all-to-all-start.3 = ((bf16[16,16,256]{2,1,0:T(8,128)(2,1)}), bf16[16,16,256]{2,1,0:T(8,128)(2,1)S(1)}, u32[]{:S(2)}, u32[]{:S(2)}) async-start(bf16[16,16,256]{2,1,0:T(8,128)(2,1)} %cross_rows.2), calls=%async_computation.3 | async-start | bytes 262144 | tf_op jit(solution)/shard_map/all_to_all | solution.py:417
  274.2 0.5 mix.2.q_ref
  274.7 8.4 %all-to-all-done.3 = bf16[16,16,256]{2,1,0:T(8,128)(2,1)S(1)} async-done(((bf16[16,16,256]{2,1,0:T(8,128)(2,1)}), bf16[16,16,256]{2,1,0:T(8,128)(2,1)S(1)}, u32[]{:S(2)}, u32[]{:S(2)}) %all-to-all-start.3) | async-done | bytes 131104 | tf_op jit(solution)/shard_map/all_to_all | solution.py:417
  283.1 4.2 %plain_merge.1 = (bf16[2,256,256]{2,1,0:T(8,128)(2,1)S(1)}, bf16[256,1024]{1,0:T(8,128)(2,1)S(1)}) custom-call(bf16[256,256]{1,0:T(8,128)(2,1)S(1)} %bitcast.10, bf16[1024,256]{1,0:T(8,128)(2,1)S(1)} %get-tuple-element.16.p_hbm, bf16[1024,256]{1,0:T(8,128)(2,1)S(1)} %mix.2.q_ref), custom_call_target="tpu_custom_call" | custom-call | tf_op jit(solution)/shard_map/plain_merge/pallas_call | solution.py:268
  287.3 0.0 collective-permute-done.6.s_ref.q_ref
  287.3 0.0 collective-permute-done.5.r_ref.p_ref
  287.3 1.2 project.1
  288.5 3.4 %all-to-all-start.4 = ((bf16[16,16,512]{2,1,0:T(8,128)(2,1)}), bf16[16,16,512]{2,1,0:T(8,128)(2,1)S(1)}, u32[]{:S(2)}, u32[]{:S(2)}) async-start(bf16[16,16,512]{2,1,0:T(8,128)(2,1)} %project.1), calls=%async_computation.4 | async-start | bytes 524288 | tf_op jit(solution)/shard_map/all_to_all | solution.py:417
  291.9 3.3 collective-permute-start.7
  295.2 6.5 %collective-permute-done.7.w_ref = bf16[2,256,256]{2,1,0:T(8,128)(2,1)S(1)} collective-permute-done((bf16[2,256,256]{2,1,0:T(8,128)(2,1)S(1)}, bf16[2,256,256]{2,1,0:T(8,128)(2,1)S(1)}, u32[]{:S(2)}, u32[]{:S(2)}) %collective-permute-start.7) | collective-permute-done | bytes 262176 | tf_op jit(solution)/shard_map/ppermute | solution.py:413
  301.7 1.9 all-to-all-done.4.parts_ref
  303.6 0.9 cross_rows.3
  304.5 5.6 %all-to-all-start.5 = ((bf16[16,16,256]{2,1,0:T(8,128)(2,1)}), bf16[16,16,256]{2,1,0:T(8,128)(2,1)S(1)}, u32[]{:S(2)}, u32[]{:S(2)}) async-start(bf16[16,16,256]{2,1,0:T(8,128)(2,1)} %cross_rows.3), calls=%async_computation.5 | async-start | bytes 262144 | tf_op jit(solution)/shard_map/all_to_all | solution.py:417
  310.1 0.5 mix.3.q_ref
  310.5 8.4 %all-to-all-done.5 = bf16[16,16,256]{2,1,0:T(8,128)(2,1)S(1)} async-done(((bf16[16,16,256]{2,1,0:T(8,128)(2,1)}), bf16[16,16,256]{2,1,0:T(8,128)(2,1)S(1)}, u32[]{:S(2)}, u32[]{:S(2)}) %all-to-all-start.5) | async-done | bytes 131104 | tf_op jit(solution)/shard_map/all_to_all | solution.py:417
  319.0 4.7 %last_merge.1 = bf16[16,16,512]{2,1,0:T(8,128)(2,1)S(1)} custom-call(bf16[256,256]{1,0:T(8,128)(2,1)S(1)} %bitcast.11, bf16[256,1024]{1,0:T(8,128)(2,1)S(1)} %get-tuple-element.17.turned_ref.turned_hbm, bf16[1024,256]{1,0:T(8,128)(2,1)S(1)} %mix.3.q_ref, bf16[1024,512]{1,0:T(8,128)(2,1)} %bitcast.12), custom_call_target="tpu_custom_call" | custom-call | tf_op jit(solution)/shard_map/last_merge/pallas_call | solution.py:324
  323.7 14.3 %all_to_all.36 = bf16[16,16,512]{2,1,0:T(8,128)(2,1)S(1)} all-to-all(bf16[16,16,512]{2,1,0:T(8,128)(2,1)S(1)} %last_merge.1), channel_id=1, replica_groups=mesh['grp'=32,'vox'=16] {'vox'}, dimensions={0} | all-to-all | bytes 524288 | tf_op jit(solution)/shard_map/all_to_all | solution.py:417
  337.9 0.7 convert_reduce_fusion.1
  (1 shorter events, 0.0 us)
Async XLA Ops:
  0.0 11.0 %collective-permute-start = (bf16[1024,256]{1,0:T(8,128)(2,1)}, bf16[1024,256]{1,0:T(8,128)(2,1)S(1)}, u32[]{:S(2)}, u32[]{:S(2)}) collective-permute-start(bf16[1024,256]{1,0:T(8,128)(2,1)} %bitcast.6), channel_id=1, source_target_pairs={{0,16},{16,0},{32,48},{48,32},{64,80},{80,64},{96,112},{112,96},{1... | collective-permute-start | bytes 1572872 | tf_op jit(solution)/shard_map/ppermute | solution.py:413
  37.9 4.2 %copy-start = (bf16[1,1024,256]{2,1,0:T(8,128)(2,1)S(1)}, bf16[1,1024,256]{2,1,0:T(8,128)(2,1)}, u32[]{:S(2)}) copy-start(bf16[1,1024,256]{2,1,0:T(8,128)(2,1)} %param.2) | copy-start | bytes 1572868
  38.6 17.2 %all-to-all-start.1 = ((f32[8,80,128]{2,1,0:T(8,128)}), f32[8,80,128]{2,1,0:T(8,128)S(1)}, u32[]{:S(2)}, u32[]{:S(2)}) async-start(f32[8,80,128]{2,1,0:T(8,128)} %broadcast_in_dim.4), calls=%async_computation.1 | async-start | bytes 655360 | tf_op jit(solution)/shard_map/all_to_all | solution.py:423
  42.1 17.0 %collective-permute-start.2 = (bf16[1024,256]{1,0:T(8,128)(2,1)S(1)}, bf16[1024,256]{1,0:T(8,128)(2,1)S(1)}, u32[]{:S(2)}, u32[]{:S(2)}) collective-permute-start(bf16[1024,256]{1,0:T(8,128)(2,1)S(1)} %bitcast.8), channel_id=1, source_target_pairs={{0,48},{16,32},{32,16},{48,0},{64,112},{80,96},{96,80},{112,64},{1... | collective-permute-start | bytes 1572872 | tf_op jit(solution)/shard_map/ppermute | solution.py:413
  46.5 23.9 %collective-permute-start.3 = (bf16[1024,256]{1,0:T(8,128)(2,1)S(1)}, bf16[1024,256]{1,0:T(8,128)(2,1)S(1)}, u32[]{:S(2)}, u32[]{:S(2)}) collective-permute-start(bf16[1024,256]{1,0:T(8,128)(2,1)S(1)} %collective-permute-done.q_ref), channel_id=1, source_target_pairs={{0,48},{16,32},{32,16},{48,0},{64,112},{80,96},{96,80},{112,64},{1... | collective-permute-start | bytes 1572872 | tf_op jit(solution)/shard_map/ppermute | solution.py:413
  55.8 14.5 %collective-permute-start.1 = (f32[8,80,128]{2,1,0:T(8,128)S(1)}, f32[8,80,128]{2,1,0:T(8,128)S(1)}, u32[]{:S(2)}, u32[]{:S(2)}) collective-permute-start(f32[8,80,128]{2,1,0:T(8,128)S(1)} %all-to-all-done.1.mine_ref), channel_id=1, source_target_pairs={{0,1},{1,0},{2,3},{3,2},{4,5},{5,4},{6,7},{7,6},{8,9},{9,8},{10,11... | collective-permute-start | bytes 983048 | tf_op jit(solution)/shard_map/ppermute | solution.py:427
  233.0 0.7 copy-start.1
  233.7 0.7 copy-start.2
  234.4 15.5 %copy-start.3 = (bf16[2,256,256]{2,1,0:T(8,128)(2,1)S(1)}, bf16[2,256,256]{2,1,0:T(8,128)(2,1)}, u32[]{:S(2)}) copy-start(bf16[2,256,256]{2,1,0:T(8,128)(2,1)} %copy-done.2) | copy-start | bytes 786436
  234.4 31.6 %all-to-all-start.2 = ((bf16[16,16,512]{2,1,0:T(8,128)(2,1)}), bf16[16,16,512]{2,1,0:T(8,128)(2,1)S(1)}, u32[]{:S(2)}, u32[]{:S(2)}) async-start(bf16[16,16,512]{2,1,0:T(8,128)(2,1)} %copy-done.1), calls=%async_computation.2 | async-start | bytes 524288 | tf_op jit(solution)/shard_map/all_to_all | solution.py:417
  241.8 45.5 %collective-permute-start.6 = (bf16[1024,256]{1,0:T(8,128)(2,1)S(1)}, bf16[1024,256]{1,0:T(8,128)(2,1)S(1)}, u32[]{:S(2)}, u32[]{:S(2)}) collective-permute-start(bf16[1024,256]{1,0:T(8,128)(2,1)S(1)} %get-tuple-element.16.p_hbm), channel_id=1, source_target_pairs={{0,112},{16,96},{32,80},{48,64},{64,48},{80,32},{96,16},{112,0},{1... | collective-permute-start | bytes 1572872 | tf_op jit(solution)/shard_map/ppermute | solution.py:413
  248.0 39.3 %collective-permute-start.5 = (bf16[1024,256]{1,0:T(8,128)(2,1)S(1)}, bf16[1024,256]{1,0:T(8,128)(2,1)S(1)}, u32[]{:S(2)}, u32[]{:S(2)}) collective-permute-start(bf16[1024,256]{1,0:T(8,128)(2,1)S(1)} %get-tuple-element.16.p_hbm), channel_id=1, source_target_pairs={{0,64},{16,80},{32,96},{48,112},{64,0},{80,16},{96,32},{112,48},{1... | collective-permute-start | bytes 1572872 | tf_op jit(solution)/shard_map/ppermute | solution.py:413
  249.9 16.1 %collective-permute-start.4 = (bf16[2,256,256]{2,1,0:T(8,128)(2,1)S(1)}, bf16[2,256,256]{2,1,0:T(8,128)(2,1)S(1)}, u32[]{:S(2)}, u32[]{:S(2)}) collective-permute-start(bf16[2,256,256]{2,1,0:T(8,128)(2,1)S(1)} %copy-done.3), channel_id=1, source_target_pairs={{0,48},{16,32},{32,16},{48,0},{64,112},{80,96},{96,80},{112,64},{1... | collective-permute-start | bytes 786440 | tf_op jit(solution)/shard_map/ppermute | solution.py:413
  266.9 16.2 %all-to-all-start.3 = ((bf16[16,16,256]{2,1,0:T(8,128)(2,1)}), bf16[16,16,256]{2,1,0:T(8,128)(2,1)S(1)}, u32[]{:S(2)}, u32[]{:S(2)}) async-start(bf16[16,16,256]{2,1,0:T(8,128)(2,1)} %cross_rows.2), calls=%async_computation.3 | async-start | bytes 262144 | tf_op jit(solution)/shard_map/all_to_all | solution.py:417
  288.5 15.1 %all-to-all-start.4 = ((bf16[16,16,512]{2,1,0:T(8,128)(2,1)}), bf16[16,16,512]{2,1,0:T(8,128)(2,1)S(1)}, u32[]{:S(2)}, u32[]{:S(2)}) async-start(bf16[16,16,512]{2,1,0:T(8,128)(2,1)} %project.1), calls=%async_computation.4 | async-start | bytes 524288 | tf_op jit(solution)/shard_map/all_to_all | solution.py:417
  291.9 9.8 %collective-permute-start.7 = (bf16[2,256,256]{2,1,0:T(8,128)(2,1)S(1)}, bf16[2,256,256]{2,1,0:T(8,128)(2,1)S(1)}, u32[]{:S(2)}, u32[]{:S(2)}) collective-permute-start(bf16[2,256,256]{2,1,0:T(8,128)(2,1)S(1)} %get-tuple-element.18), channel_id=1, source_target_pairs={{0,64},{16,80},{32,96},{48,112},{64,0},{80,16},{96,32},{112,48},{1... | collective-permute-start | bytes 786440 | tf_op jit(solution)/shard_map/ppermute | solution.py:413
  304.5 14.5 %all-to-all-start.5 = ((bf16[16,16,256]{2,1,0:T(8,128)(2,1)}), bf16[16,16,256]{2,1,0:T(8,128)(2,1)S(1)}, u32[]{:S(2)}, u32[]{:S(2)}) async-start(bf16[16,16,256]{2,1,0:T(8,128)(2,1)} %cross_rows.3), calls=%async_computation.5 | async-start | bytes 262144 | tf_op jit(solution)/shard_map/all_to_all | solution.py:417
where the time goes:
time: 339 us
  Pallas kernels  178 us (53%)
  waiting for transfers between devices  64.1 us (19%)
  starting transfers between devices  53.4 us (16%)
  blocking collectives  40.4 us (12%)
    pallas_call x1, Pallas kernels, full_merge(): pl.pallas_call(full_kernel, out_shape=(WEIGHTS, jax.ShapeDtypeStruct(p.sh...  163 us
    all_to_all x2, blocking collectives, exchange(): return lax.all_to_all(parts, 'vox', 0, 0)  40.4 us
    ppermute x7, waiting for transfers between devices, partner(): return lax.ppermute(value, 'grp', [(g, g ^ mask) for g in range(GRP)])  38.1 us
    ppermute x7, starting transfers between devices, partner(): return lax.ppermute(value, 'grp', [(g, g ^ mask) for g in range(GRP)])  24 us
    all_to_all x4, starting transfers between devices, exchange(): return lax.all_to_all(parts, 'vox', 0, 0)  23.7 us
    all_to_all x4, waiting for transfers between devices, exchange(): return lax.all_to_all(parts, 'vox', 0, 0)  18.7 us
    all_to_all x1, waiting for transfers between devices, same_core(): return lax.all_to_all(sent, 'vox', 0, 0, axis_index_groups=groups)  7.22 us
  transfers between devices with their start and end apart: 13, of which 9 were waited for; matrix products, arithmetic and copies ran while one was open for 0% of the time, Pallas kernels for 2%

commit v1 on v0

--- a/solution.py
+++ b/solution.py
@@ -367,25 +367,21 @@
     )(pltpu.with_memory_space_constraint(p, pltpu.MemorySpace.HBM))
 
 
-def pair_gram_kernel(turned_ref, q_ref, own_ref, out_ref):
-    q = q_ref[...]
-    out_ref[:, :24, :] = own_ref[...]
-    for k, block in enumerate(lower_blocks(q.T, q)):
-        out_ref[:, 24 + 8 * k : 32 + 8 * k, :] = block.astype(BF16).reshape(VOX, 8, H)
+def cross_gram_kernel(turned_ref, q_ref, out_ref):
     for k in range(2):
-        got = dot1(turned_ref[...], q[:, H * k : H * (k + 1)], NN).astype(BF16)
-        out_ref[:, 48 + ROWS * k : 64 + ROWS * k, :] = got.reshape(VOX, ROWS, H)
-
-
-def pair_gram(turned, q, own):
-    return pl.pallas_call(
-        pair_gram_kernel,
-        out_shape=jax.ShapeDtypeStruct((VOX, 80, H), BF16),
-        in_specs=[VMEM] * 3,
+        got = dot1(turned_ref[...], q_ref[:, H * k : H * (k + 1)], NN).astype(BF16)
+        out_ref[:, ROWS * k : ROWS * (k + 1), :] = got.reshape(VOX, ROWS, H)
+
+
+def cross_gram(turned, q):
+    return pl.pallas_call(
+        cross_gram_kernel,
+        out_shape=jax.ShapeDtypeStruct((VOX, 2 * ROWS, H), BF16),
+        in_specs=[VMEM] * 2,
         out_specs=VMEM,
-        compiler_params=params(8),
-        name="pair_gram",
-    )(turned, q, own)
+        compiler_params=params(6),
+        name="cross_gram",
+    )(turned, q)
 
 
 def rows_kernel(parts_ref, w_ref, out_ref):
@@ -437,8 +433,10 @@
     turned, own_parts = self_gram(own)
     far_own = partner(own, 3)
     far_other = partner(other, 3)
-    parts = pair_gram(turned, other, own_parts)
-    rows = add_up(exchange(parts))
+    own_rows = add_up(exchange(own_parts))
+    other_rows = partner(own_rows, 1)
+    cross_rows = add_up(exchange(cross_gram(turned, other)))
+    rows = jnp.concatenate([own_rows, other_rows, cross_rows], axis=0)
     mine = same_core(rows)
     theirs = swap_cores(mine)
     w, left, parts = full_merge(core, mine, theirs, own, other, far_own, far_other)

time: 339 us -> 336 us (level)
  blocking collectives: 40.4 us -> 14.3 us
  starting transfers between devices: 53.4 us -> 70.2 us
  waiting for transfers between devices: 64.1 us -> 69.2 us
    all_to_all x2 -> x1, blocking collectives: 40.4 us -> 14.3 us  [exchange(): return lax.all_to_all(parts, 'vox', 0, 0)]
    all_to_all x4 -> x6, starting transfers between devices: 23.7 us -> 36.5 us  [exchange(): return lax.all_to_all(parts, 'vox', 0, 0)]
    all_to_all x4 -> x6, waiting for transfers between devices: 18.7 us -> 30.6 us  [exchange(): return lax.all_to_all(parts, 'vox', 0, 0)]
    ppermute x7 -> x8, waiting for transfers between devices: 38.1 us -> 31.5 us  [partner(): return lax.ppermute(value, 'grp', [(g, g ^ mask) for g in range(GRP)])]
    ppermute x7 -> x8, starting transfers between devices: 24 us -> 27.8 us  [partner(): return lax.ppermute(value, 'grp', [(g, g ^ mask) for g in range(GRP)])]
  transfers between devices with their start and end apart: 13 -> 16, of which waited for: 9 -> 9; matrix products, arithmetic and copies ran while one was open for 0% -> 0% of each run, Pallas kernels for 2% -> 3%
where the time goes in v1:
time: 336 us; the launch traced here: 335 us
  Pallas kernels  179 us (53%)
  starting transfers between devices  70.2 us (21%)
  waiting for transfers between devices  69.2 us (21%)
  blocking collectives  14.3 us (4%)
    pallas_call x1, Pallas kernels, full_merge(): pl.pallas_call(full_kernel, out_shape=(WEIGHTS, jax.ShapeDtypeStruct(p.sh...  163 us
    all_to_all x6, starting transfers between devices, exchange(): return lax.all_to_all(parts, 'vox', 0, 0)  36.5 us
    ppermute x8, waiting for transfers between devices, partner(): return lax.ppermute(value, 'grp', [(g, g ^ mask) for g in range(GRP)])  31.5 us
    all_to_all x6, waiting for transfers between devices, exchange(): return lax.all_to_all(parts, 'vox', 0, 0)  30.6 us
    ppermute x8, starting transfers between devices, partner(): return lax.ppermute(value, 'grp', [(g, g ^ mask) for g in range(GRP)])  27.8 us
    all_to_all x1, blocking collectives, exchange(): return lax.all_to_all(parts, 'vox', 0, 0)  14.3 us
    all_to_all x1, waiting for transfers between devices, same_core(): return lax.all_to_all(sent, 'vox', 0, 0, axis_index_groups=groups)  7.08 us
  transfers between devices with their start and end apart: 16, of which 9 were waited for; matrix products, arithmetic and copies ran while one was open for 0% of the time, Pallas kernels for 3%

profile of v1, /device:TPU:1, one launch (start us, length us, event | category | flops | bytes accessed | tf_op | source)
XLA Modules:
  0.0 335.3 jit_solution(7411514998118426684)
XLA Ops:
  0.0 3.9 %collective-permute-start.1 = (bf16[1024,256]{1,0:T(8,128)(2,1)}, bf16[1024,256]{1,0:T(8,128)(2,1)S(1)}, u32[]{:S(2)}, u32[]{:S(2)}) collective-permute-start(bf16[1024,256]{1,0:T(8,128)(2,1)} %bitcast.6), channel_id=1, source_target_pairs={{0,16},{16,0},{32,48},{48,32},{64,80},{80,64},{96,112},{112,96},{1... | collective-permute-start | bytes 1572872 | tf_op jit(solution)/shard_map/ppermute | solution.py:409
  3.9 2.1 self_gram.1
  6.0 8.1 %all-to-all-start = ((bf16[16,24,128]{2,1,0:T(8,128)(2,1)}), bf16[16,24,128]{2,1,0:T(8,128)(2,1)S(1)}, u32[]{:S(2)}, u32[]{:S(2)}) async-start(bf16[16,24,128]{2,1,0:T(8,128)(2,1)} %get-tuple-element.12), calls=%async_computation | async-start | bytes 196608 | tf_op jit(solution)/shard_map/all_to_all | solution.py:413
  14.2 0.0 collective-permute-done.1.q_ref
  14.2 1.1 cross_gram.1
  15.2 7.4 %all-to-all-done = bf16[16,24,128]{2,1,0:T(8,128)(2,1)S(1)} async-done(((bf16[16,24,128]{2,1,0:T(8,128)(2,1)}), bf16[16,24,128]{2,1,0:T(8,128)(2,1)S(1)}, u32[]{:S(2)}, u32[]{:S(2)}) %all-to-all-start) | async-done | bytes 98336 | tf_op jit(solution)/shard_map/all_to_all | solution.py:413
  22.7 3.4 %all-to-all-start.1 = ((bf16[16,32,128]{2,1,0:T(8,128)(2,1)}), bf16[16,32,128]{2,1,0:T(8,128)(2,1)S(1)}, u32[]{:S(2)}, u32[]{:S(2)}) async-start(bf16[16,32,128]{2,1,0:T(8,128)(2,1)} %cross_gram.1), calls=%async_computation.1 | async-start | bytes 262144 | tf_op jit(solution)/shard_map/all_to_all | solution.py:413
  26.1 3.6 %collective-permute-start = (f32[24,128]{1,0:T(8,128)S(1)}, f32[24,128]{1,0:T(8,128)S(1)}, u32[]{:S(2)}, u32[]{:S(2)}) collective-permute-start(f32[24,128]{1,0:T(8,128)S(1)} %convert_reduce_fusion.2), channel_id=1, source_target_pairs={{0,16},{16,0},{32,48},{48,32},{64,80},{80,64},{96,112},{112,96},{1... | collective-permute-start | bytes 36872 | tf_op jit(solution)/shard_map/ppermute | solution.py:409
  29.8 5.0 %all-to-all-done.1 = bf16[16,32,128]{2,1,0:T(8,128)(2,1)S(1)} async-done(((bf16[16,32,128]{2,1,0:T(8,128)(2,1)}), bf16[16,32,128]{2,1,0:T(8,128)(2,1)S(1)}, u32[]{:S(2)}, u32[]{:S(2)}) %all-to-all-start.1) | async-done | bytes 131104 | tf_op jit(solution)/shard_map/all_to_all | solution.py:413
  34.8 0.0 collective-permute-done
  34.8 0.0 copy-start
  34.8 0.8 broadcast_in_dim.4
  35.6 3.4 %all-to-all-start.2 = ((f32[8,80,128]{2,1,0:T(8,128)}), f32[8,80,128]{2,1,0:T(8,128)S(1)}, u32[]{:S(2)}, u32[]{:S(2)}) async-start(f32[8,80,128]{2,1,0:T(8,128)} %broadcast_in_dim.4), calls=%async_computation.2 | async-start | bytes 655360 | tf_op jit(solution)/shard_map/all_to_all | solution.py:419
  39.0 4.0 %collective-permute-start.3 = (bf16[1024,256]{1,0:T(8,128)(2,1)S(1)}, bf16[1024,256]{1,0:T(8,128)(2,1)S(1)}, u32[]{:S(2)}, u32[]{:S(2)}) collective-permute-start(bf16[1024,256]{1,0:T(8,128)(2,1)S(1)} %bitcast.8), channel_id=1, source_target_pairs={{0,48},{16,32},{32,16},{48,0},{64,112},{80,96},{96,80},{112,64},{1... | collective-permute-start | bytes 1572872 | tf_op jit(solution)/shard_map/ppermute | solution.py:409
  43.0 2.5 collective-permute-start.4
  45.5 7.1 %all-to-all-done.2.mine_ref = f32[8,80,128]{2,1,0:T(8,128)S(1)} async-done(((f32[8,80,128]{2,1,0:T(8,128)}), f32[8,80,128]{2,1,0:T(8,128)S(1)}, u32[]{:S(2)}, u32[]{:S(2)}) %all-to-all-start.2) | async-done | bytes 327712 | tf_op jit(solution)/shard_map/all_to_all | solution.py:419
  52.6 2.5 collective-permute-start.2
  55.1 0.0 collective-permute-done.3.r_ref.p_ref
  55.1 11.2 %collective-permute-done.4.s_ref.q_ref = bf16[1024,256]{1,0:T(8,128)(2,1)S(1)} collective-permute-done((bf16[1024,256]{1,0:T(8,128)(2,1)S(1)}, bf16[1024,256]{1,0:T(8,128)(2,1)S(1)}, u32[]{:S(2)}, u32[]{:S(2)}) %collective-permute-start.4) | collective-permute-done | bytes 524320 | tf_op jit(solution)/shard_map/ppermute | solution.py:409
  66.3 0.0 collective-permute-done.2.theirs_ref
  66.3 162.7 %full_merge.1 = (bf16[2,256,256]{2,1,0:T(8,128)(2,1)S(1)}, bf16[1024,256]{1,0:T(8,128)(2,1)S(1)}, bf16[16,16,512]{2,1,0:T(8,128)(2,1)S(1)}) custom-call(s32[1]{0:T(128)} %bitcast.core_ref, f32[8,80,128]{2,1,0:T(8,128)S(1)} %all-to-all-done.2.mine_ref, f32[8,80,128]{2,1,0:T(8,128)S(1)} %collective-permute-done.2.theirs_ref, bf16[1024,256]{1,0:T(8,128)(2,1)S(1)} %bitcast.9, ...), custom_call_target="tpu_custom_call" | custom-call | tf_op jit(solution)/shard_map/full_merge/pallas_call | solution.py:245
  229.0 0.7 copy-done.1
  229.7 0.7 copy-done.2
  230.4 8.4 %all-to-all-start.3 = ((bf16[16,16,512]{2,1,0:T(8,128)(2,1)}), bf16[16,16,512]{2,1,0:T(8,128)(2,1)S(1)}, u32[]{:S(2)}, u32[]{:S(2)}) async-start(bf16[16,16,512]{2,1,0:T(8,128)(2,1)} %copy-done.1), calls=%async_computation.3 | async-start | bytes 524288 | tf_op jit(solution)/shard_map/all_to_all | solution.py:413
  238.7 5.8 %collective-permute-start.7 = (bf16[1024,256]{1,0:T(8,128)(2,1)S(1)}, bf16[1024,256]{1,0:T(8,128)(2,1)S(1)}, u32[]{:S(2)}, u32[]{:S(2)}) collective-permute-start(bf16[1024,256]{1,0:T(8,128)(2,1)S(1)} %get-tuple-element.16.p_hbm), channel_id=1, source_target_pairs={{0,112},{16,96},{32,80},{48,64},{64,48},{80,32},{96,16},{112,0},{1... | collective-permute-start | bytes 1572872 | tf_op jit(solution)/shard_map/ppermute | solution.py:409
  244.5 1.9 collective-permute-start.6
  246.4 2.5 collective-permute-start.5
  248.9 13.6 %collective-permute-done.5.w_ref = bf16[2,256,256]{2,1,0:T(8,128)(2,1)S(1)} collective-permute-done((bf16[2,256,256]{2,1,0:T(8,128)(2,1)S(1)}, bf16[2,256,256]{2,1,0:T(8,128)(2,1)S(1)}, u32[]{:S(2)}, u32[]{:S(2)}) %collective-permute-start.5) | collective-permute-done | bytes 262176 | tf_op jit(solution)/shard_map/ppermute | solution.py:409
  262.5 0.0 all-to-all-done.3.parts_ref
  262.5 0.9 cross_rows.2
  263.4 7.3 %all-to-all-start.4 = ((bf16[16,16,256]{2,1,0:T(8,128)(2,1)}), bf16[16,16,256]{2,1,0:T(8,128)(2,1)S(1)}, u32[]{:S(2)}, u32[]{:S(2)}) async-start(bf16[16,16,256]{2,1,0:T(8,128)(2,1)} %cross_rows.2), calls=%async_computation.4 | async-start | bytes 262144 | tf_op jit(solution)/shard_map/all_to_all | solution.py:413
  270.7 0.5 mix.2.q_ref
  271.2 8.4 %all-to-all-done.4 = bf16[16,16,256]{2,1,0:T(8,128)(2,1)S(1)} async-done(((bf16[16,16,256]{2,1,0:T(8,128)(2,1)}), bf16[16,16,256]{2,1,0:T(8,128)(2,1)S(1)}, u32[]{:S(2)}, u32[]{:S(2)}) %all-to-all-start.4) | async-done | bytes 131104 | tf_op jit(solution)/shard_map/all_to_all | solution.py:413
  279.6 4.2 %plain_merge.1 = (bf16[2,256,256]{2,1,0:T(8,128)(2,1)S(1)}, bf16[256,1024]{1,0:T(8,128)(2,1)S(1)}) custom-call(bf16[256,256]{1,0:T(8,128)(2,1)S(1)} %bitcast.10, bf16[1024,256]{1,0:T(8,128)(2,1)S(1)} %get-tuple-element.16.p_hbm, bf16[1024,256]{1,0:T(8,128)(2,1)S(1)} %mix.2.q_ref), custom_call_target="tpu_custom_call" | custom-call | tf_op jit(solution)/shard_map/plain_merge/pallas_call | solution.py:268
  283.8 0.0 collective-permute-done.7.s_ref.q_ref
  283.8 0.0 collective-permute-done.6.r_ref.p_ref
  283.8 1.1 project.1
  285.0 3.4 %all-to-all-start.5 = ((bf16[16,16,512]{2,1,0:T(8,128)(2,1)}), bf16[16,16,512]{2,1,0:T(8,128)(2,1)S(1)}, u32[]{:S(2)}, u32[]{:S(2)}) async-start(bf16[16,16,512]{2,1,0:T(8,128)(2,1)} %project.1), calls=%async_computation.5 | async-start | bytes 524288 | tf_op jit(solution)/shard_map/all_to_all | solution.py:413
  288.4 3.6 %collective-permute-start.8 = (bf16[2,256,256]{2,1,0:T(8,128)(2,1)S(1)}, bf16[2,256,256]{2,1,0:T(8,128)(2,1)S(1)}, u32[]{:S(2)}, u32[]{:S(2)}) collective-permute-start(bf16[2,256,256]{2,1,0:T(8,128)(2,1)S(1)} %get-tuple-element.18), channel_id=1, source_target_pairs={{0,64},{16,80},{32,96},{48,112},{64,0},{80,16},{96,32},{112,48},{1... | collective-permute-start | bytes 786440 | tf_op jit(solution)/shard_map/ppermute | solution.py:409
  292.1 6.7 %collective-permute-done.8.w_ref = bf16[2,256,256]{2,1,0:T(8,128)(2,1)S(1)} collective-permute-done((bf16[2,256,256]{2,1,0:T(8,128)(2,1)S(1)}, bf16[2,256,256]{2,1,0:T(8,128)(2,1)S(1)}, u32[]{:S(2)}, u32[]{:S(2)}) %collective-permute-start.8) | collective-permute-done | bytes 262176 | tf_op jit(solution)/shard_map/ppermute | solution.py:409
  298.8 1.3 all-to-all-done.5.parts_ref
  300.1 0.9 cross_rows.3
  301.0 5.9 %all-to-all-start.6 = ((bf16[16,16,256]{2,1,0:T(8,128)(2,1)}), bf16[16,16,256]{2,1,0:T(8,128)(2,1)S(1)}, u32[]{:S(2)}, u32[]{:S(2)}) async-start(bf16[16,16,256]{2,1,0:T(8,128)(2,1)} %cross_rows.3), calls=%async_computation.6 | async-start | bytes 262144 | tf_op jit(solution)/shard_map/all_to_all | solution.py:413
  306.8 0.5 mix.3.q_ref
  307.3 8.4 %all-to-all-done.6 = bf16[16,16,256]{2,1,0:T(8,128)(2,1)S(1)} async-done(((bf16[16,16,256]{2,1,0:T(8,128)(2,1)}), bf16[16,16,256]{2,1,0:T(8,128)(2,1)S(1)}, u32[]{:S(2)}, u32[]{:S(2)}) %all-to-all-start.6) | async-done | bytes 131104 | tf_op jit(solution)/shard_map/all_to_all | solution.py:413
  315.7 4.7 %last_merge.1 = bf16[16,16,512]{2,1,0:T(8,128)(2,1)S(1)} custom-call(bf16[256,256]{1,0:T(8,128)(2,1)S(1)} %bitcast.11, bf16[256,1024]{1,0:T(8,128)(2,1)S(1)} %get-tuple-element.17.turned_ref.turned_hbm, bf16[1024,256]{1,0:T(8,128)(2,1)S(1)} %mix.3.q_ref, bf16[1024,512]{1,0:T(8,128)(2,1)} %bitcast.12), custom_call_target="tpu_custom_call" | custom-call | tf_op jit(solution)/shard_map/last_merge/pallas_call | solution.py:324
  320.4 14.3 %all_to_all.40 = bf16[16,16,512]{2,1,0:T(8,128)(2,1)S(1)} all-to-all(bf16[16,16,512]{2,1,0:T(8,128)(2,1)S(1)} %last_merge.1), channel_id=1, replica_groups=mesh['grp'=32,'vox'=16] {'vox'}, dimensions={0} | all-to-all | bytes 524288 | tf_op jit(solution)/shard_map/all_to_all | solution.py:413
  334.7 0.7 convert_reduce_fusion
  (8 shorter events, 0.1 us)
Async XLA Ops:
  0.0 14.2 %collective-permute-start.1 = (bf16[1024,256]{1,0:T(8,128)(2,1)}, bf16[1024,256]{1,0:T(8,128)(2,1)S(1)}, u32[]{:S(2)}, u32[]{:S(2)}) collective-permute-start(bf16[1024,256]{1,0:T(8,128)(2,1)} %bitcast.6), channel_id=1, source_target_pairs={{0,16},{16,0},{32,48},{48,32},{64,80},{80,64},{96,112},{112,96},{1... | collective-permute-start | bytes 1572872 | tf_op jit(solution)/shard_map/ppermute | solution.py:409
  6.0 16.6 %all-to-all-start = ((bf16[16,24,128]{2,1,0:T(8,128)(2,1)}), bf16[16,24,128]{2,1,0:T(8,128)(2,1)S(1)}, u32[]{:S(2)}, u32[]{:S(2)}) async-start(bf16[16,24,128]{2,1,0:T(8,128)(2,1)} %get-tuple-element.12), calls=%async_computation | async-start | bytes 196608 | tf_op jit(solution)/shard_map/all_to_all | solution.py:413
  22.7 12.1 %all-to-all-start.1 = ((bf16[16,32,128]{2,1,0:T(8,128)(2,1)}), bf16[16,32,128]{2,1,0:T(8,128)(2,1)S(1)}, u32[]{:S(2)}, u32[]{:S(2)}) async-start(bf16[16,32,128]{2,1,0:T(8,128)(2,1)} %cross_gram.1), calls=%async_computation.1 | async-start | bytes 262144 | tf_op jit(solution)/shard_map/all_to_all | solution.py:413
  26.1 8.7 %collective-permute-start = (f32[24,128]{1,0:T(8,128)S(1)}, f32[24,128]{1,0:T(8,128)S(1)}, u32[]{:S(2)}, u32[]{:S(2)}) collective-permute-start(f32[24,128]{1,0:T(8,128)S(1)} %convert_reduce_fusion.2), channel_id=1, source_target_pairs={{0,16},{16,0},{32,48},{48,32},{64,80},{80,64},{96,112},{112,96},{1... | collective-permute-start | bytes 36872 | tf_op jit(solution)/shard_map/ppermute | solution.py:409
  34.8 4.2 %copy-start = (bf16[1,1024,256]{2,1,0:T(8,128)(2,1)S(1)}, bf16[1,1024,256]{2,1,0:T(8,128)(2,1)}, u32[]{:S(2)}) copy-start(bf16[1,1024,256]{2,1,0:T(8,128)(2,1)} %param.2) | copy-start | bytes 1572868
  35.6 17.0 %all-to-all-start.2 = ((f32[8,80,128]{2,1,0:T(8,128)}), f32[8,80,128]{2,1,0:T(8,128)S(1)}, u32[]{:S(2)}, u32[]{:S(2)}) async-start(f32[8,80,128]{2,1,0:T(8,128)} %broadcast_in_dim.4), calls=%async_computation.2 | async-start | bytes 655360 | tf_op jit(solution)/shard_map/all_to_all | solution.py:419
  39.0 16.1 %collective-permute-start.3 = (bf16[1024,256]{1,0:T(8,128)(2,1)S(1)}, bf16[1024,256]{1,0:T(8,128)(2,1)S(1)}, u32[]{:S(2)}, u32[]{:S(2)}) collective-permute-start(bf16[1024,256]{1,0:T(8,128)(2,1)S(1)} %bitcast.8), channel_id=1, source_target_pairs={{0,48},{16,32},{32,16},{48,0},{64,112},{80,96},{96,80},{112,64},{1... | collective-permute-start | bytes 1572872 | tf_op jit(solution)/shard_map/ppermute | solution.py:409
  43.0 23.3 %collective-permute-start.4 = (bf16[1024,256]{1,0:T(8,128)(2,1)S(1)}, bf16[1024,256]{1,0:T(8,128)(2,1)S(1)}, u32[]{:S(2)}, u32[]{:S(2)}) collective-permute-start(bf16[1024,256]{1,0:T(8,128)(2,1)S(1)} %collective-permute-done.1.q_ref), channel_id=1, source_target_pairs={{0,48},{16,32},{32,16},{48,0},{64,112},{80,96},{96,80},{112,64},{1... | collective-permute-start | bytes 1572872 | tf_op jit(solution)/shard_map/ppermute | solution.py:409
  52.6 13.7 %collective-permute-start.2 = (f32[8,80,128]{2,1,0:T(8,128)S(1)}, f32[8,80,128]{2,1,0:T(8,128)S(1)}, u32[]{:S(2)}, u32[]{:S(2)}) collective-permute-start(f32[8,80,128]{2,1,0:T(8,128)S(1)} %all-to-all-done.2.mine_ref), channel_id=1, source_target_pairs={{0,1},{1,0},{2,3},{3,2},{4,5},{5,4},{6,7},{7,6},{8,9},{9,8},{10,11... | collective-permute-start | bytes 983048 | tf_op jit(solution)/shard_map/ppermute | solution.py:423
  229.0 0.7 copy-start.1
  229.7 0.7 copy-start.2
  230.4 16.0 %copy-start.3 = (bf16[2,256,256]{2,1,0:T(8,128)(2,1)S(1)}, bf16[2,256,256]{2,1,0:T(8,128)(2,1)}, u32[]{:S(2)}) copy-start(bf16[2,256,256]{2,1,0:T(8,128)(2,1)} %copy-done.2) | copy-start | bytes 786436
  230.4 32.1 %all-to-all-start.3 = ((bf16[16,16,512]{2,1,0:T(8,128)(2,1)}), bf16[16,16,512]{2,1,0:T(8,128)(2,1)S(1)}, u32[]{:S(2)}, u32[]{:S(2)}) async-start(bf16[16,16,512]{2,1,0:T(8,128)(2,1)} %copy-done.1), calls=%async_computation.3 | async-start | bytes 524288 | tf_op jit(solution)/shard_map/all_to_all | solution.py:413
  238.7 45.1 %collective-permute-start.7 = (bf16[1024,256]{1,0:T(8,128)(2,1)S(1)}, bf16[1024,256]{1,0:T(8,128)(2,1)S(1)}, u32[]{:S(2)}, u32[]{:S(2)}) collective-permute-start(bf16[1024,256]{1,0:T(8,128)(2,1)S(1)} %get-tuple-element.16.p_hbm), channel_id=1, source_target_pairs={{0,112},{16,96},{32,80},{48,64},{64,48},{80,32},{96,16},{112,0},{1... | collective-permute-start | bytes 1572872 | tf_op jit(solution)/shard_map/ppermute | solution.py:409
  244.5 39.3 %collective-permute-start.6 = (bf16[1024,256]{1,0:T(8,128)(2,1)S(1)}, bf16[1024,256]{1,0:T(8,128)(2,1)S(1)}, u32[]{:S(2)}, u32[]{:S(2)}) collective-permute-start(bf16[1024,256]{1,0:T(8,128)(2,1)S(1)} %get-tuple-element.16.p_hbm), channel_id=1, source_target_pairs={{0,64},{16,80},{32,96},{48,112},{64,0},{80,16},{96,32},{112,48},{1... | collective-permute-start | bytes 1572872 | tf_op jit(solution)/shard_map/ppermute | solution.py:409
  246.4 16.1 %collective-permute-start.5 = (bf16[2,256,256]{2,1,0:T(8,128)(2,1)S(1)}, bf16[2,256,256]{2,1,0:T(8,128)(2,1)S(1)}, u32[]{:S(2)}, u32[]{:S(2)}) collective-permute-start(bf16[2,256,256]{2,1,0:T(8,128)(2,1)S(1)} %copy-done.3), channel_id=1, source_target_pairs={{0,48},{16,32},{32,16},{48,0},{64,112},{80,96},{96,80},{112,64},{1... | collective-permute-start | bytes 786440 | tf_op jit(solution)/shard_map/ppermute | solution.py:409
  263.4 16.2 %all-to-all-start.4 = ((bf16[16,16,256]{2,1,0:T(8,128)(2,1)}), bf16[16,16,256]{2,1,0:T(8,128)(2,1)S(1)}, u32[]{:S(2)}, u32[]{:S(2)}) async-start(bf16[16,16,256]{2,1,0:T(8,128)(2,1)} %cross_rows.2), calls=%async_computation.4 | async-start | bytes 262144 | tf_op jit(solution)/shard_map/all_to_all | solution.py:413
  285.0 15.1 %all-to-all-start.5 = ((bf16[16,16,512]{2,1,0:T(8,128)(2,1)}), bf16[16,16,512]{2,1,0:T(8,128)(2,1)S(1)}, u32[]{:S(2)}, u32[]{:S(2)}) async-start(bf16[16,16,512]{2,1,0:T(8,128)(2,1)} %project.1), calls=%async_computation.5 | async-start | bytes 524288 | tf_op jit(solution)/shard_map/all_to_all | solution.py:413
  288.4 10.3 %collective-permute-start.8 = (bf16[2,256,256]{2,1,0:T(8,128)(2,1)S(1)}, bf16[2,256,256]{2,1,0:T(8,128)(2,1)S(1)}, u32[]{:S(2)}, u32[]{:S(2)}) collective-permute-start(bf16[2,256,256]{2,1,0:T(8,128)(2,1)S(1)} %get-tuple-element.18), channel_id=1, source_target_pairs={{0,64},{16,80},{32,96},{48,112},{64,0},{80,16},{96,32},{112,48},{1... | collective-permute-start | bytes 786440 | tf_op jit(solution)/shard_map/ppermute | solution.py:409
  301.0 14.7 %all-to-all-start.6 = ((bf16[16,16,256]{2,1,0:T(8,128)(2,1)}), bf16[16,16,256]{2,1,0:T(8,128)(2,1)S(1)}, u32[]{:S(2)}, u32[]{:S(2)}) async-start(bf16[16,16,256]{2,1,0:T(8,128)(2,1)} %cross_rows.3), calls=%async_computation.6 | async-start | bytes 262144 | tf_op jit(solution)/shard_map/all_to_all | solution.py:413
